TPU v7x, 32 devices: a whole 2x2x4 slice. The times are simulated.
32 devices in a mesh: layer: 16 (over z, x, core), row: 2 (over y).
Axes of the slice: x: 2, y: 2, z: 4, core: 2. Of those that a mesh axis runs over, the one named last changes fastest.
Arguments:
- waves: bfloat16 [16, 3072, 512], P('layer', 'row'), may hold values from -6 to 6
- operators: bfloat16 [16, 4, 3072, 3072], P('layer', None, 'row'), may hold values from -0.0546875 to 0.0546875
- sources: bfloat16 [3072, 512], P('row'), may hold values from -6 to 6
- source_layer: int32 [128], replicated, may hold values from 0 to 15
Outputs:
- traces: bfloat16 [16, 3072, 512], P('layer', 'row')
All inputs are finite; a program needn't handle non-finite values.
Results may differ from a plain program's by a relative error of at most 0.0057.
Values may be sent and summed in bfloat16 or wider, within the bound.
A program may use at most 128 MiB of HBM per device.

v0:
```python
import functools
import math

import jax
import jax.numpy as jnp
from jax import lax
from jax.experimental import pallas as pl
from jax.experimental.pallas import tpu as pltpu
from jax.sharding import PartitionSpec as P

TICKS = 3
RELAY = 4
MESH = pl.DeviceIdType.MESH


def swap_halves(first, second):
    half = first.shape[1] // 2
    low = lax.broadcasted_iota(jnp.int32, first.shape, 1) < half
    return (
        jnp.where(low, first, pltpu.roll(second, half, 1)),
        jnp.where(low, pltpu.roll(first, half, 1), second),
    )


def kernel(
    layers, row_parts, chunk, big,
    waves, operators, sources, source_layer, traces,
    held, current, turned, total, outgoing, final, source_term, stage,
    stage_sem, load_sem, store_sem, row_send, send_sem, recv_sem, final_sem,
):
    layer = lax.axis_index("layer")
    part = lax.axis_index("row")
    rows, lanes = outgoing.shape[3], outgoing.shape[4]
    depth = current.shape[3]
    chunks = rows // chunk
    has_above, has_below = layer > 0, layer < layers - 1

    def piece(i, size=chunk, base=0):
        return pl.ds(pl.multiple_of(base + i * size, chunk), size)

    def load(i):
        span = piece(i, big)
        return pltpu.make_async_copy(operators.at[0, :, span, :], held.at[:, span, :], load_sem.at[i])

    wave_load = pltpu.make_async_copy(waves.at[0], stage, stage_sem.at[0])
    source_load = pltpu.make_async_copy(sources, stage, stage_sem.at[1])
    wave_load.start()

    barrier = pltpu.get_barrier_semaphore()
    for d in range(1, row_parts):
        pl.semaphore_signal(barrier, inc=1, device_id=(layer, lax.rem(part + d, row_parts)), device_id_type=MESH)
    for present, other in ((has_above, layer - 1), (has_below, layer + 1)):
        @pl.when(present)
        def _():
            pl.semaphore_signal(barrier, inc=1, device_id=(other, part), device_id_type=MESH)

    wave_load.wait()
    for i in range(rows // big):
        load(i).start()

    def packed(span):
        for way in range(2):
            at = 2 * way * lanes
            re = stage[span, at:at + lanes].astype(jnp.float32)
            im = stage[span, at + lanes:at + 2 * lanes].astype(jnp.float32)
            yield way, swap_halves(re, im)

    own_base = part * rows

    peers = row_parts - 1 + has_above.astype(jnp.int32) + has_below.astype(jnp.int32)
    pl.semaphore_wait(barrier, peers)

    def forward(tick, group, way, span):
        for d in range(1, row_parts):
            pltpu.make_async_remote_copy(
                src_ref=current.at[tick, group, way, span, :],
                dst_ref=current.at[tick, group, way, span, :],
                send_sem=row_send.at[tick, group, way, d - 1],
                recv_sem=recv_sem.at[tick, group, way, part],
                device_id=(layer, lax.rem(part + d, row_parts)),
                device_id_type=MESH,
            ).start()

    @pl.loop(0, chunks)
    def _(i):
        span = piece(i, chunk, own_base)
        for way, groups in packed(piece(i)):
            for group in range(2):
                current[0, group, way, span, :] = groups[group].astype(jnp.bfloat16)
        forward(0, 0, 0, span)
        forward(0, 0, 1, span)

    own = piece(0, rows, own_base)
    forward(0, 1, 0, own)
    forward(0, 1, 1, own)

    source_load.start()
    source_load.wait()
    mask = (source_layer[...] == layer).astype(jnp.float32)
    pair = jnp.concatenate([mask, mask], 1)
    packed_mask = swap_halves(pair[:, :lanes], pair[:, lanes:])

    @pl.loop(0, chunks)
    def _(i):
        for way, groups in packed(piece(i)):
            for group in range(2):
                source_term[group, way, piece(i), :] = (groups[group] * packed_mask[group]).astype(jnp.bfloat16)

    for way, present in ((0, has_above), (1, has_below)):
        @pl.when(jnp.logical_not(present))
        def _():
            for group in range(2):
                final[group, way] = jnp.zeros((rows, lanes), jnp.bfloat16)
                for tick in range(1, TICKS):
                    @pl.loop(0, depth // chunk)
                    def _(i):
                        current[tick, group, way, piece(i), :] = jnp.zeros((chunk, lanes), jnp.bfloat16)

    def arrived(tick, group, way, p):
        ref = current.at[tick, group, way, piece(0, rows, p * rows), :]
        pltpu.make_async_copy(ref, ref, recv_sem.at[tick, group, way, p]).wait()

    def product(tick, group, span, inner):
        down, up = current[tick, group, 0, inner, :], current[tick, group, 1, inner, :]
        down_turned, up_turned = turned[0], turned[1]
        out = jnp.dot(held[0, span, inner], jnp.concatenate([down, up], 1), preferred_element_type=jnp.float32)
        out += jnp.dot(held[1, span, inner], jnp.concatenate([down_turned, up_turned], 1), preferred_element_type=jnp.float32)
        out += jnp.dot(held[2, span, inner], jnp.concatenate([up, down], 1), preferred_element_type=jnp.float32)
        out += jnp.dot(held[3, span, inner], jnp.concatenate([up_turned, down_turned], 1), preferred_element_type=jnp.float32)
        return out

    def take_next(step):
        tick, group = step // 2, step % 2
        for way, present in ((0, has_above), (1, has_below)):
            @pl.when(jnp.logical_and(present, jnp.logical_and(step >= 2, step < 2 * TICKS)))
            def _():
                arrived(tick, group, way, part)
                forward(tick, group, way, own)

    @pl.loop(0, 2 * TICKS)
    def _(step):
        tick, group = step // 2, step % 2
        for d in range(row_parts):
            p = lax.rem(part + d, row_parts)
            inner = pl.ds(pl.multiple_of(p * rows, 128), rows)
            if d == min(1, row_parts - 1):
                take_next(step + 1)

            if d > 0:
                @pl.when(tick == 0)
                def _():
                    arrived(tick, group, 0, p)
                    arrived(tick, group, 1, p)

                for way, present in ((0, has_above), (1, has_below)):
                    @pl.when(jnp.logical_and(tick > 0, present))
                    def _():
                        arrived(tick, group, way, p)

            @pl.loop(0, chunks)
            def _(i):
                low = lax.broadcasted_iota(jnp.int32, (chunk, lanes), 1) < lanes // 2
                for way in range(2):
                    block = current[tick, group, way, piece(i, chunk, p * rows), :]
                    rolled = pltpu.roll(block.astype(jnp.float32), lanes // 2, 1)
                    turned[way, piece(i), :] = jnp.where(low, -rolled, rolled).astype(jnp.bfloat16)

            if d < row_parts - 1:
                @pl.loop(0, rows // big)
                def _(i):
                    span = piece(i, big)
                    if d == 0:
                        @pl.when(step == 0)
                        def _():
                            load(i).wait()
                        total[span, :] = product(tick, group, span, inner)
                    else:
                        total[span, :] += product(tick, group, span, inner)
                continue

            @pl.loop(0, chunks)
            def _(i):
                span = piece(i)
                if row_parts == 1:
                    @pl.when(jnp.logical_and(step == 0, i % (big // chunk) == 0))
                    def _():
                        load(i // (big // chunk)).wait()
                out = product(tick, group, span, inner)
                if row_parts > 1:
                    out += total[span, :]
                for way in range(2):
                    value = out[:, way * lanes:(way + 1) * lanes] + source_term[group, way, span, :].astype(jnp.float32)
                    outgoing[tick, group, way, span, :] = value.astype(jnp.bfloat16)

                there = piece(i, chunk, own_base)
                for way, present, other in ((0, has_below, layer + 1), (1, has_above, layer - 1)):
                    @pl.when(jnp.logical_and(present, tick < TICKS - 1))
                    def _():
                        pltpu.make_async_remote_copy(
                            src_ref=outgoing.at[tick, group, way, span, :],
                            dst_ref=current.at[tick + 1, group, way, there, :],
                            send_sem=send_sem.at[tick, group, way],
                            recv_sem=recv_sem.at[tick + 1, group, way, part],
                            device_id=(other, part),
                            device_id_type=MESH,
                        ).start()

                    @pl.when(jnp.logical_and(present, tick == TICKS - 1))
                    def _():
                        pltpu.make_async_remote_copy(
                            src_ref=outgoing.at[tick, group, way, span, :],
                            dst_ref=final.at[group, way, span, :],
                            send_sem=send_sem.at[tick, group, way],
                            recv_sem=final_sem.at[group, way, i],
                            device_id=(other, part),
                            device_id_type=MESH,
                        ).start()

    def store(i):
        return pltpu.make_async_copy(stage.at[piece(i), :], traces.at[0, piece(i), :], store_sem.at[i])

    @pl.loop(0, chunks)
    def _(i):
        span = piece(i)
        for way, present in ((0, has_above), (1, has_below)):
            @pl.when(present)
            def _():
                for group in range(2):
                    ref = final.at[group, way, span, :]
                    pltpu.make_async_copy(ref, ref, final_sem.at[group, way, i]).wait()
            a = final[0, way, span, :].astype(jnp.float32)
            b = final[1, way, span, :].astype(jnp.float32)
            for q, block in enumerate(swap_halves(a, b)):
                at = (2 * way + q) * lanes
                stage[span, at:at + lanes] = block.astype(jnp.bfloat16)
        store(i).start()

    def sent(tick, group, way):
        for d in range(1, row_parts):
            ref = current.at[tick, group, way, own, :]
            pltpu.make_async_copy(ref, ref, row_send.at[tick, group, way, d - 1]).wait()

    for group in range(2):
        for way, came, goes in ((0, has_above, has_below), (1, has_below, has_above)):
            sent(0, group, way)

            @pl.when(came)
            def _():
                for tick in range(1, TICKS):
                    sent(tick, group, way)

            @pl.when(goes)
            def _():
                for tick in range(TICKS):
                    ref = outgoing.at[tick, group, way]
                    pltpu.make_async_copy(ref, ref, send_sem.at[tick, group, way]).wait()

    for i in range(chunks):
        store(i).wait()


def relay(traces, result, buffer, in_sem, out_sem):
    size = traces.shape[1] // RELAY
    spans = [pl.ds(i * size, size) for i in range(RELAY)]
    takes = [pltpu.make_async_copy(traces.at[:, s], buffer.at[:, s], in_sem.at[i]) for i, s in enumerate(spans)]
    puts = [pltpu.make_async_copy(buffer.at[:, s], result.at[:, s], out_sem.at[i]) for i, s in enumerate(spans)]
    for take in takes:
        take.start()
    for take, put in zip(takes, puts):
        take.wait()
        put.start()
    for put in puts:
        put.wait()


def per_device(waves, operators, sources, source_layer):
    layers, row_parts = lax.axis_size("layer"), lax.axis_size("row")
    rows, depth = operators.shape[2], operators.shape[3]
    lanes = waves.shape[2] // 4
    chunk, big = math.gcd(rows, 256), math.gcd(rows, 512)
    anywhere = pl.BlockSpec(memory_space=pl.ANY)
    traces = pl.pallas_call(
        functools.partial(kernel, layers, row_parts, chunk, big),
        out_shape=jax.ShapeDtypeStruct(waves.shape, jnp.bfloat16),
        in_specs=[anywhere, anywhere, anywhere, pl.BlockSpec(memory_space=pltpu.VMEM)],
        out_specs=anywhere,
        scratch_shapes=[
            pltpu.VMEM((4, rows, depth), jnp.bfloat16),
            pltpu.VMEM((TICKS, 2, 2, depth, lanes), jnp.bfloat16),
            pltpu.VMEM((2, rows, lanes), jnp.bfloat16),
            pltpu.VMEM((rows, 2 * lanes), jnp.float32),
            pltpu.VMEM((TICKS, 2, 2, rows, lanes), jnp.bfloat16),
            pltpu.VMEM((2, 2, rows, lanes), jnp.bfloat16),
            pltpu.VMEM((2, 2, rows, lanes), jnp.bfloat16),
            pltpu.VMEM((rows, 4 * lanes), jnp.bfloat16),
            pltpu.SemaphoreType.DMA((2,)),
            pltpu.SemaphoreType.DMA((rows // big,)),
            pltpu.SemaphoreType.DMA((rows // chunk,)),
            pltpu.SemaphoreType.DMA((TICKS, 2, 2, max(row_parts - 1, 1))),
            pltpu.SemaphoreType.DMA((TICKS, 2, 2)),
            pltpu.SemaphoreType.DMA((TICKS, 2, 2, row_parts)),
            pltpu.SemaphoreType.DMA((2, 2, rows // chunk)),
        ],
        compiler_params=pltpu.CompilerParams(
            collective_id=0, has_side_effects=True, vmem_limit_bytes=67043328
        ),
    )(waves, operators, sources, source_layer.reshape(1, lanes))
    return pl.pallas_call(
        relay,
        out_shape=jax.ShapeDtypeStruct(traces.shape, traces.dtype),
        in_specs=[anywhere],
        out_specs=anywhere,
        scratch_shapes=[
            pltpu.VMEM(traces.shape, traces.dtype),
            pltpu.SemaphoreType.DMA((RELAY,)),
            pltpu.SemaphoreType.DMA((RELAY,)),
        ],
    )(traces)


def solution(mesh):
    return jax.shard_map(
        per_device,
        mesh=mesh,
        in_specs=(P("layer", "row", None), P("layer", None, "row", None), P("row", None), P()),
        out_specs=P("layer", "row", None),
        check_vma=False,
    )
```

profile of v0, /device:TPU:17, one launch (start us, length us, event | category | flops | bytes accessed | tf_op | source)
XLA Modules:
  0.0 122.0 jit_solution(9431029383019701466)
XLA Ops:
  0.0 119.8 %shard_map.46.traces = bf16[1,1536,512]{2,1,0:T(8,128)(2,1)} custom-call(bf16[1,1536,512]{2,1,0:T(8,128)(2,1)} %waves.1, bf16[1,4,1536,3072]{3,2,1,0:T(8,128)(2,1)} %operators.1, bf16[1536,512]{1,0:T(8,128)(2,1)} %sources.1, s32[1,128]{1,0:T(1,128)} %bitcast.1), custom_call_target="tpu_custom_call" | custom-call | tf_op jit(solution)/shard_map/pallas_call | solution.py:282
  119.8 2.2 %shard_map.47 = bf16[1,1536,512]{2,1,0:T(8,128)(2,1)} custom-call(bf16[1,1536,512]{2,1,0:T(8,128)(2,1)} %shard_map.46.traces), custom_call_target="tpu_custom_call" | custom-call | tf_op jit(solution)/shard_map/pallas_call | solution.py:308
where the time goes:
time: 122 us
  Pallas kernels  122 us (100%)
    pallas_call x1, Pallas kernels, per_device(): pl.pallas_call(functools.partial(kernel, layers, row_parts, chunk, big),...  120 us

commit v1 on v0

v1 whole, which is shorter than its diff:
```python
import functools
import math

import jax
import jax.numpy as jnp
from jax import lax
from jax.experimental import pallas as pl
from jax.experimental.pallas import tpu as pltpu
from jax.sharding import PartitionSpec as P

TICKS = 3
LAST = TICKS - 1
MESH = pl.DeviceIdType.MESH


def swap_halves(first, second):
    half = first.shape[1] // 2
    low = lax.broadcasted_iota(jnp.int32, first.shape, 1) < half
    return (
        jnp.where(low, first, pltpu.roll(second, half, 1)),
        jnp.where(low, pltpu.roll(first, half, 1), second),
    )


def even_quarter(shape):
    return jnp.bitwise_and(lax.broadcasted_iota(jnp.int32, shape, 1), shape[1] // 4) == 0


def swap_quarters(first, second):
    quarter = first.shape[1] // 4
    even = even_quarter(first.shape)
    return (
        jnp.where(even, first, pltpu.roll(second, quarter, 1)),
        jnp.where(even, pltpu.roll(first, 3 * quarter, 1), second),
    )


def turn(block):
    half = block.shape[1] // 2
    rolled = pltpu.roll(block, half, 1)
    return jnp.where(lax.broadcasted_iota(jnp.int32, block.shape, 1) < half, -rolled, rolled)


def exchange_quarters(block):
    quarter = block.shape[1] // 4
    return jnp.where(even_quarter(block.shape), pltpu.roll(block, 3 * quarter, 1), pltpu.roll(block, quarter, 1))


def kernel(
    layers, row_parts, chunk, big, deep, tall,
    waves, operators, sources, source_layer, final, final_sub,
    held, current, turned, total, outgoing, source_term, stage, sub, spun, total_sub, outgoing_sub,
    wave_sem, source_sem, load_sem, zero_sem, row_send, send_sem, recv_sem, final_sem,
    sub_send, sub_recv, last_send, last_recv,
):
    layer = lax.axis_index("layer")
    part = lax.axis_index("row")
    rows, lanes = outgoing.shape[2], outgoing.shape[3]
    depth = current.shape[3]
    chunks, deeps = rows // chunk, rows // deep
    pair = chunk // 2
    has_above, has_below = layer > 0, layer < layers - 1

    def piece(i, size=chunk, base=0):
        return pl.ds(pl.multiple_of(base + i * size, math.gcd(size, rows)), size)

    def load(i):
        span = piece(i, big)
        return pltpu.make_async_copy(operators.at[0, :, span, :], held.at[:, span, :], load_sem.at[i])

    def wave_load(i):
        return pltpu.make_async_copy(waves.at[0, piece(i), :], stage.at[piece(i), :], wave_sem.at[i])

    source_load = pltpu.make_async_copy(sources, stage, source_sem.at[0])
    for i in range(chunks):
        wave_load(i).start()

    barrier = pltpu.get_barrier_semaphore()
    for d in range(1, row_parts):
        pl.semaphore_signal(barrier, inc=1, device_id=(layer, lax.rem(part + d, row_parts)), device_id_type=MESH)
    for present, other in ((has_above, layer - 1), (has_below, layer + 1)):
        @pl.when(present)
        def _():
            pl.semaphore_signal(barrier, inc=1, device_id=(other, part), device_id_type=MESH)

    for i in range(rows // big):
        load(i).start()

    def packed(span):
        for way in range(2):
            at = 2 * way * lanes
            re = stage[span, at:at + lanes].astype(jnp.float32)
            im = stage[span, at + lanes:at + 2 * lanes].astype(jnp.float32)
            yield way, swap_halves(re, im)

    own_base = part * rows

    peers = row_parts - 1 + has_above.astype(jnp.int32) + has_below.astype(jnp.int32)
    pl.semaphore_wait(barrier, peers)

    def forward(tick, group, way, span):
        for d in range(1, row_parts):
            pltpu.make_async_remote_copy(
                src_ref=current.at[tick, group, way, span, :],
                dst_ref=current.at[tick, group, way, span, :],
                send_sem=row_send.at[tick, group, way, d - 1],
                recv_sem=recv_sem.at[tick, group, way, part],
                device_id=(layer, lax.rem(part + d, row_parts)),
                device_id_type=MESH,
            ).start()

    @pl.loop(0, chunks)
    def _(i):
        wave_load(i).wait()
        span = piece(i, chunk, own_base)
        for way, groups in packed(piece(i)):
            for group in range(2):
                current[0, group, way, span, :] = groups[group].astype(jnp.bfloat16)
        forward(0, 0, 0, span)
        forward(0, 0, 1, span)

    own = piece(0, rows, own_base)
    forward(0, 1, 0, own)
    forward(0, 1, 1, own)

    source_load.start()
    source_load.wait()
    mask = (source_layer[...] == layer).astype(jnp.float32)
    both = jnp.concatenate([mask, mask], 1)
    packed_mask = swap_halves(both[:, :lanes], both[:, lanes:])

    @pl.loop(0, chunks)
    def _(i):
        for way, groups in packed(piece(i)):
            for group in range(2):
                source_term[group, way, piece(i), :] = (groups[group] * packed_mask[group]).astype(jnp.bfloat16)

    def zero_final(way):
        empty = current.at[1, 0, way]
        yield pltpu.make_async_copy(empty.at[pl.ds(0, rows), :], final.at[way], zero_sem.at[way, 0])
        for q in range(2):
            yield pltpu.make_async_copy(empty.at[pl.ds(0, rows // 2), :], final_sub.at[q, way], zero_sem.at[way, 1 + q])

    for way, present in ((0, has_above), (1, has_below)):
        @pl.when(jnp.logical_not(present))
        def _():
            for group in range(2):
                for tick in range(1, TICKS):
                    @pl.loop(0, depth // chunk)
                    def _(i):
                        current[tick, group, way, piece(i), :] = jnp.zeros((chunk, lanes), jnp.bfloat16)
            for copy in zero_final(way):
                copy.start()

    def arrived(tick, group, way, p):
        ref = current.at[tick, group, way, piece(0, rows, p * rows), :]
        pltpu.make_async_copy(ref, ref, recv_sem.at[tick, group, way, p]).wait()

    def product(tick, group, span, inner):
        down, up = current[tick, group, 0, inner, :], current[tick, group, 1, inner, :]
        down_turned, up_turned = turned[0], turned[1]
        out = jnp.dot(held[0, span, inner], jnp.concatenate([down, up], 1), preferred_element_type=jnp.float32)
        out += jnp.dot(held[1, span, inner], jnp.concatenate([down_turned, up_turned], 1), preferred_element_type=jnp.float32)
        out += jnp.dot(held[2, span, inner], jnp.concatenate([up, down], 1), preferred_element_type=jnp.float32)
        out += jnp.dot(held[3, span, inner], jnp.concatenate([up_turned, down_turned], 1), preferred_element_type=jnp.float32)
        return out

    def part_of(d):
        p = lax.rem(part + d, row_parts)
        return p, pl.ds(pl.multiple_of(p * rows, 128), rows)

    def turn_part(tick, group, p):
        @pl.loop(0, chunks)
        def _(i):
            for way in range(2):
                block = current[tick, group, way, piece(i, chunk, p * rows), :].astype(jnp.float32)
                turned[way, piece(i), :] = turn(block).astype(jnp.bfloat16)

    def own_half(tick, group, first):
        p, inner = part_of(0)
        turn_part(tick, group, p)

        @pl.loop(0, rows // big)
        def _(i):
            @pl.when(first)
            def _():
                load(i).wait()
            total[piece(i, big), :] = product(tick, group, piece(i, big), inner)

    def other_half(tick, group, send):
        for d in range(1, row_parts):
            p, inner = part_of(d)
            for way, present in ((0, has_above), (1, has_below)):
                @pl.when(jnp.logical_or(tick == 0, present))
                def _():
                    arrived(tick, group, way, p)
            turn_part(tick, group, p)
            if d < row_parts - 1:
                @pl.loop(0, rows // big)
                def _(i):
                    span = piece(i, big)
                    total[span, :] += product(tick, group, span, inner)
                continue

            @pl.loop(0, chunks)
            def _(i):
                span = piece(i)
                out = product(tick, group, span, inner) + total[span, :]
                step = 2 * tick + group
                for way in range(2):
                    value = out[:, way * lanes:(way + 1) * lanes] + source_term[group, way, span, :].astype(jnp.float32)
                    outgoing[step, way, span, :] = value.astype(jnp.bfloat16)
                send(step, span, piece(i, chunk, own_base))

    ways = ((0, has_below, layer + 1), (1, has_above, layer - 1))

    def send_next(step, span, there):
        tick, group = step // 2, step % 2
        for way, present, other in ways:
            @pl.when(present)
            def _():
                pltpu.make_async_remote_copy(
                    src_ref=outgoing.at[step, way, span, :],
                    dst_ref=current.at[tick + 1, group, way, there, :],
                    send_sem=send_sem.at[step, way],
                    recv_sem=recv_sem.at[tick + 1, group, way, part],
                    device_id=(other, part),
                    device_id_type=MESH,
                ).start()

    def send_final(step, span, there):
        for way, present, other in ways:
            @pl.when(present)
            def _():
                pltpu.make_async_remote_copy(
                    src_ref=outgoing.at[step, way, span, :],
                    dst_ref=final.at[way, span, :],
                    send_sem=send_sem.at[step, way],
                    recv_sem=final_sem.at[way],
                    device_id=(other, part),
                    device_id_type=MESH,
                ).start()

    def take_next(step):
        tick, group = step // 2, step % 2
        for way, present in ((0, has_above), (1, has_below)):
            @pl.when(jnp.logical_and(present, step >= 2))
            def _():
                arrived(tick, group, way, part)
                forward(tick, group, way, own)

    def take_sub():
        for way, present in ((0, has_above), (1, has_below)):
            @pl.when(present)
            def _():
                arrived(LAST, 1, way, part)

        @pl.loop(0, chunks)
        def _(i):
            span = piece(i, chunk, own_base)
            down = current[LAST, 1, 0, span, :].astype(jnp.float32)
            up = current[LAST, 1, 1, span, :].astype(jnp.float32)
            for q, block in enumerate(swap_quarters(down, up)):
                sub[q, span, :] = block.astype(jnp.bfloat16)

        for q in range(2):
            for k in range(deeps):
                for d in range(1, row_parts):
                    span = piece(k, deep, own_base)
                    pltpu.make_async_remote_copy(
                        src_ref=sub.at[q, span, :],
                        dst_ref=sub.at[q, span, :],
                        send_sem=sub_send.at[q, d - 1],
                        recv_sem=sub_recv.at[q, k, part],
                        device_id=(layer, lax.rem(part + d, row_parts)),
                        device_id_type=MESH,
                    ).start()

    def own_sub():
        p, inner = part_of(0)
        turn_part(LAST, 1, p)

        @pl.loop(0, rows // big)
        def _(i):
            span = piece(i, big)
            out = product(LAST, 1, span, inner)
            sides = [
                out[:, way * lanes:(way + 1) * lanes] + source_term[1, way, span, :].astype(jnp.float32)
                for way in range(2)
            ]
            for q, block in enumerate(swap_quarters(*sides)):
                total_sub[q, span, :] = block

    def take_block(q, p, k):
        span = piece(k, deep, p * rows)
        ref = sub.at[q, span, :]
        pltpu.make_async_copy(ref, ref, sub_recv.at[q, k, p]).wait()
        block = sub[q, span, :].astype(jnp.float32)
        swapped = exchange_quarters(block)
        for n, value in enumerate((turn(block), swapped, turn(swapped))):
            spun[n] = value.astype(jnp.bfloat16)

    def product_sub(q, p, k, span):
        inner = pl.ds(pl.multiple_of(p * rows + k * deep, 128), deep)
        out = jnp.dot(held[0, span, inner], sub[q, inner, :], preferred_element_type=jnp.float32)
        for n in range(3):
            out += jnp.dot(held[1 + n, span, inner], spun[n], preferred_element_type=jnp.float32)
        return out + total_sub[q, span, :]

    def other_sub(q):
        for d in range(1, row_parts):
            p = lax.rem(part + d, row_parts)
            done = deeps if d < row_parts - 1 else deeps - 1

            if done:
                @pl.loop(0, done)
                def _(k):
                    take_block(q, p, k)

                    @pl.loop(0, rows // tall)
                    def _(i):
                        span = piece(i, tall)
                        total_sub[q, span, :] = product_sub(q, p, k, span)

        take_block(q, p, deeps - 1)

        @pl.loop(0, chunks)
        def _(i):
            out = product_sub(q, p, deeps - 1, piece(i))
            here = piece(i, pair)
            for (way, present, other), block in zip(ways, swap_quarters(out[:pair], out[pair:])):
                outgoing_sub[q, way, here, :] = block.astype(jnp.bfloat16)

                @pl.when(present)
                def _():
                    pltpu.make_async_remote_copy(
                        src_ref=outgoing_sub.at[q, way, here, :],
                        dst_ref=final_sub.at[q, way, here, :],
                        send_sem=last_send.at[q, way],
                        recv_sem=last_recv.at[q, way],
                        device_id=(other, part),
                        device_id_type=MESH,
                    ).start()

    @pl.loop(0, 2 * LAST)
    def _(step):
        tick, group = step // 2, step % 2
        own_half(tick, group, step == 0)
        take_next(step + 1)
        other_half(tick, group, send_next)

    own_half(LAST, 0, layer < 0)
    take_sub()
    own_sub()
    other_half(LAST, 0, send_final)
    for q in range(2):
        other_sub(q)

    def whole(ref, sem):
        pltpu.make_async_copy(ref, ref, sem).wait()

    for way, came, goes in ((0, has_above, has_below), (1, has_below, has_above)):
        def sent(tick, group):
            for d in range(1, row_parts):
                whole(current.at[tick, group, way, own, :], row_send.at[tick, group, way, d - 1])

        for group in range(2):
            sent(0, group)

        @pl.when(came)
        def _():
            for step in range(2, 2 * LAST + 1):
                sent(step // 2, step % 2)
            whole(final.at[way], final_sem.at[way])
            for q in range(2):
                whole(final_sub.at[q, way], last_recv.at[q, way])

        @pl.when(jnp.logical_not(came))
        def _():
            for copy in zero_final(way):
                copy.wait()

        @pl.when(goes)
        def _():
            for step in range(2 * LAST + 1):
                whole(outgoing.at[step, way], send_sem.at[step, way])
            for q in range(2):
                whole(outgoing_sub.at[q, way], last_send.at[q, way])

    for q in range(2):
        for d in range(1, row_parts):
            whole(sub.at[q, own, :], sub_send.at[q, d - 1])


def unpack(chunk, final, final_sub, result, first, second, natural, first_sem, second_sem, out_sem):
    rows, lanes = first.shape[1], first.shape[2]
    pair = chunk // 2
    chunks = rows // chunk

    def takes(i):
        full, half = pl.ds(i * chunk, chunk), pl.ds(i * pair, pair)
        return (
            pltpu.make_async_copy(final.at[:, full, :], first.at[:, full, :], first_sem.at[i]),
            pltpu.make_async_copy(final_sub.at[:, :, half, :], second.at[:, :, half, :], second_sem.at[i]),
        )

    def put(i):
        full = pl.ds(i * chunk, chunk)
        return pltpu.make_async_copy(natural.at[full, :], result.at[0, full, :], out_sem.at[i])

    for i in range(chunks):
        for copy in takes(i):
            copy.start()
    for i in range(chunks):
        for copy in takes(i):
            copy.wait()
        full, half = pl.ds(i * chunk, chunk), pl.ds(i * pair, pair)
        for way in range(2):
            a = first[way, full, :].astype(jnp.float32)
            b = jnp.concatenate(
                swap_quarters(second[0, way, half, :].astype(jnp.float32), second[1, way, half, :].astype(jnp.float32)), 0
            )
            for n, block in enumerate(swap_halves(a, b)):
                at = (2 * way + n) * lanes
                natural[full, at:at + lanes] = block.astype(jnp.bfloat16)
        put(i).start()
    for i in range(chunks):
        put(i).wait()


def per_device(waves, operators, sources, source_layer):
    layers, row_parts = lax.axis_size("layer"), lax.axis_size("row")
    rows, depth = operators.shape[2], operators.shape[3]
    lanes = waves.shape[2] // 4
    chunk, big, deep, tall = (math.gcd(rows, size) for size in (256, 512, 384, 768))
    chunks, steps = rows // chunk, 2 * LAST + 1
    peers = row_parts - 1
    anywhere = pl.BlockSpec(memory_space=pl.ANY)
    dma = pltpu.SemaphoreType.DMA
    final, final_sub = pl.pallas_call(
        functools.partial(kernel, layers, row_parts, chunk, big, deep, tall),
        out_shape=(
            jax.ShapeDtypeStruct((2, rows, lanes), jnp.bfloat16),
            jax.ShapeDtypeStruct((2, 2, rows // 2, lanes), jnp.bfloat16),
        ),
        in_specs=[anywhere, anywhere, anywhere, pl.BlockSpec(memory_space=pltpu.VMEM)],
        out_specs=(anywhere, anywhere),
        scratch_shapes=[
            pltpu.VMEM((4, rows, depth), jnp.bfloat16),
            pltpu.VMEM((TICKS, 2, 2, depth, lanes), jnp.bfloat16),
            pltpu.VMEM((2, rows, lanes), jnp.bfloat16),
            pltpu.VMEM((rows, 2 * lanes), jnp.float32),
            pltpu.VMEM((steps, 2, rows, lanes), jnp.bfloat16),
            pltpu.VMEM((2, 2, rows, lanes), jnp.bfloat16),
            pltpu.VMEM((rows, 4 * lanes), jnp.bfloat16),
            pltpu.VMEM((2, depth, lanes), jnp.bfloat16),
            pltpu.VMEM((3, deep, lanes), jnp.bfloat16),
            pltpu.VMEM((2, rows, lanes), jnp.float32),
            pltpu.VMEM((2, 2, rows // 2, lanes), jnp.bfloat16),
            dma((chunks,)),
            dma((1,)),
            dma((rows // big,)),
            dma((2, 3)),
            dma((TICKS, 2, 2, peers)),
            dma((steps, 2)),
            dma((TICKS, 2, 2, row_parts)),
            dma((2,)),
            dma((2, peers)),
            dma((2, rows // deep, row_parts)),
            dma((2, 2)),
            dma((2, 2)),
        ],
        compiler_params=pltpu.CompilerParams(
            collective_id=0, has_side_effects=True, vmem_limit_bytes=67043328
        ),
    )(waves, operators, sources, source_layer.reshape(1, lanes))
    return pl.pallas_call(
        functools.partial(unpack, chunk),
        out_shape=jax.ShapeDtypeStruct(waves.shape, jnp.bfloat16),
        in_specs=[anywhere, anywhere],
        out_specs=anywhere,
        scratch_shapes=[
            pltpu.VMEM(final.shape, jnp.bfloat16),
            pltpu.VMEM(final_sub.shape, jnp.bfloat16),
            pltpu.VMEM((rows, 4 * lanes), jnp.bfloat16),
            dma((chunks,)),
            dma((chunks,)),
            dma((chunks,)),
        ],
    )(final, final_sub)


def solution(mesh):
    return jax.shard_map(
        per_device,
        mesh=mesh,
        in_specs=(P("layer", "row", None), P("layer", None, "row", None), P("row", None), P()),
        out_specs=P("layer", "row", None),
        check_vma=False,
    )
```

time: 122 us -> 124 us (1.016)
  Pallas kernels: 122 us -> 124 us
    pallas_call x2, Pallas kernels: 122 us -> 124 us  [the longest x1 121 us: per_device(): pl.pallas_call(functools.partial(kernel, layers, row_parts, chunk, big, d...]
where the time goes in v1:
time: 124 us
  Pallas kernels  124 us (100%)
    pallas_call x1, Pallas kernels, per_device(): pl.pallas_call(functools.partial(kernel, layers, row_parts, chunk, big, d...  121 us
    pallas_call x1, Pallas kernels, per_device(): pl.pallas_call(functools.partial(unpack, chunk), out_shape=jax.ShapeDtype...  3.1 us

profile of v1, /device:TPU:17, one launch (start us, length us, event | category | flops | bytes accessed | tf_op | source)
XLA Modules:
  0.0 123.7 jit_solution(15306694829402214101)
XLA Ops:
  0.0 120.6 %shard_map.46 = (bf16[2,1536,128]{2,1,0:T(8,128)(2,1)}, bf16[2,2,768,128]{3,2,1,0:T(8,128)(2,1)}) custom-call(bf16[1,1536,512]{2,1,0:T(8,128)(2,1)} %waves.1, bf16[1,4,1536,3072]{3,2,1,0:T(8,128)(2,1)} %operators.1, bf16[1536,512]{1,0:T(8,128)(2,1)} %sources.1, s32[1,128]{1,0:T(1,128)} %bitcast.1), custom_call_target="tpu_custom_call" | custom-call | tf_op jit(solution)/shard_map/pallas_call | solution.py:440
  120.6 3.1 %shard_map.47 = bf16[1,1536,512]{2,1,0:T(8,128)(2,1)} custom-call(bf16[2,1536,128]{2,1,0:T(8,128)(2,1)} %get-tuple-element.7.final, bf16[2,2,768,128]{3,2,1,0:T(8,128)(2,1)} %get-tuple-element.8.final_sub), custom_call_target="tpu_custom_call" | custom-call | tf_op jit(solution)/shard_map/pallas_call | solution.py:477

commit v2 on v1

v2 whole, which is shorter than its diff:
```python
import functools
import math

import jax
import jax.numpy as jnp
from jax import lax
from jax.experimental import pallas as pl
from jax.experimental.pallas import tpu as pltpu
from jax.sharding import PartitionSpec as P

TICKS = 3
LAST = TICKS - 1
MESH = pl.DeviceIdType.MESH


def swap_halves(first, second):
    half = first.shape[1] // 2
    low = lax.broadcasted_iota(jnp.int32, first.shape, 1) < half
    return (
        jnp.where(low, first, pltpu.roll(second, half, 1)),
        jnp.where(low, pltpu.roll(first, half, 1), second),
    )


def even_quarter(shape):
    return jnp.bitwise_and(lax.broadcasted_iota(jnp.int32, shape, 1), shape[1] // 4) == 0


def swap_quarters(first, second):
    quarter = first.shape[1] // 4
    even = even_quarter(first.shape)
    return (
        jnp.where(even, first, pltpu.roll(second, quarter, 1)),
        jnp.where(even, pltpu.roll(first, 3 * quarter, 1), second),
    )


def turn(block):
    half = block.shape[1] // 2
    rolled = pltpu.roll(block, half, 1)
    return jnp.where(lax.broadcasted_iota(jnp.int32, block.shape, 1) < half, -rolled, rolled)


def exchange_quarters(block):
    quarter = block.shape[1] // 4
    return jnp.where(even_quarter(block.shape), pltpu.roll(block, 3 * quarter, 1), pltpu.roll(block, quarter, 1))


def kernel(
    layers, row_parts, fine, chunk, big, tall, slim, joint, deep, early,
    waves, operators, sources, source_layer, final, final_sub,
    held, current, turned, total, outgoing, source_term, stage, sub,
    wave_sem, source_sem, load_sem, zero_sem, row_send, send_sem, recv_sem, final_sem,
    block_recv, sub_send, sub_recv, last_send, last_recv, *relay_refs,
):
    layer = lax.axis_index("layer")
    part = lax.axis_index("row")
    rows, lanes = outgoing.shape[2], outgoing.shape[3]
    depth = current.shape[3]
    pieces, chunks = rows // fine, rows // chunk
    pair = slim // 2
    unit = math.gcd(math.gcd(fine, pair), deep)
    blocks = ([(joint, rows - joint)], [(start, deep) for start in range(joint, rows, deep)])
    left = rows - joint
    has_above, has_below = layer > 0, layer < layers - 1

    def piece(i, size=fine, base=0):
        return pl.ds(pl.multiple_of(base + i * size, unit), size)

    def load(i):
        span = piece(i, big)
        return pltpu.make_async_copy(operators.at[0, :, span, :], held.at[:, span, :], load_sem.at[i])

    def wave_load(i):
        return pltpu.make_async_copy(waves.at[0, piece(i), :], stage.at[piece(i), :], wave_sem.at[i])

    source_load = pltpu.make_async_copy(sources, stage, source_sem.at[0])
    for i in range(pieces):
        wave_load(i).start()

    barrier = pltpu.get_barrier_semaphore()
    for d in range(1, row_parts):
        pl.semaphore_signal(barrier, inc=1, device_id=(layer, lax.rem(part + d, row_parts)), device_id_type=MESH)
    for present, other in ((has_above, layer - 1), (has_below, layer + 1)):
        @pl.when(present)
        def _():
            pl.semaphore_signal(barrier, inc=1, device_id=(other, part), device_id_type=MESH)

    for i in range(rows // big):
        load(i).start()

    def packed(span):
        for way in range(2):
            at = 2 * way * lanes
            re = stage[span, at:at + lanes].astype(jnp.float32)
            im = stage[span, at + lanes:at + 2 * lanes].astype(jnp.float32)
            yield way, swap_halves(re, im)

    own_base = part * rows

    peers = row_parts - 1 + has_above.astype(jnp.int32) + has_below.astype(jnp.int32)
    pl.semaphore_wait(barrier, peers)

    def forward(tick, group, way, span, arrival=None):
        for d in range(1, row_parts):
            pltpu.make_async_remote_copy(
                src_ref=current.at[tick, group, way, span, :],
                dst_ref=current.at[tick, group, way, span, :],
                send_sem=row_send.at[tick, group, way, d - 1],
                recv_sem=recv_sem.at[tick, group, way, part] if arrival is None else arrival,
                device_id=(layer, lax.rem(part + d, row_parts)),
                device_id_type=MESH,
            ).start()

    @pl.loop(0, pieces)
    def _(i):
        wave_load(i).wait()
        span = piece(i, fine, own_base)
        for way, groups in packed(piece(i)):
            for group in range(2):
                current[0, group, way, span, :] = groups[group].astype(jnp.bfloat16)
        forward(0, 0, 0, span)
        forward(0, 0, 1, span)

    own = piece(0, rows, own_base)
    forward(0, 1, 0, own)
    forward(0, 1, 1, own)

    source_load.start()
    source_load.wait()
    mask = (source_layer[...] == layer).astype(jnp.float32)
    both = jnp.concatenate([mask, mask], 1)
    packed_mask = swap_halves(both[:, :lanes], both[:, lanes:])

    @pl.loop(0, pieces)
    def _(i):
        for way, groups in packed(piece(i)):
            for group in range(2):
                source_term[group, way, piece(i), :] = (groups[group] * packed_mask[group]).astype(jnp.bfloat16)

    def zero_final(way):
        empty = current.at[1, 0, way]
        yield pltpu.make_async_copy(empty.at[pl.ds(0, rows), :], final.at[way], zero_sem.at[way, 0])
        for q in range(2):
            yield pltpu.make_async_copy(empty.at[pl.ds(0, rows // 2), :], final_sub.at[q, way], zero_sem.at[way, 1 + q])

    for way, present in ((0, has_above), (1, has_below)):
        @pl.when(jnp.logical_not(present))
        def _():
            for group in range(2):
                for tick in range(1, TICKS):
                    @pl.loop(0, depth // fine)
                    def _(i):
                        current[tick, group, way, piece(i), :] = jnp.zeros((fine, lanes), jnp.bfloat16)
            for copy in zero_final(way):
                copy.start()

    def arrived(tick, group, way, p):
        ref = current.at[tick, group, way, piece(0, rows, p * rows), :]
        pltpu.make_async_copy(ref, ref, recv_sem.at[tick, group, way, p]).wait()

    def multiply(span, inner, columns):
        return jnp.dot(
            jnp.concatenate([held[m, span, inner] for m in range(4)], 1),
            jnp.concatenate(columns, 0),
            preferred_element_type=jnp.float32,
        )

    def product(tick, group, span, inner):
        down, up = current[tick, group, 0, inner, :], current[tick, group, 1, inner, :]
        down_turned, up_turned = turned[0, :inner.size, :], turned[1, :inner.size, :]
        columns = ((down, up), (down_turned, up_turned), (up, down), (up_turned, down_turned))
        return multiply(span, inner, [jnp.concatenate(pair_of, 1) for pair_of in columns])

    def part_of(d):
        p = lax.rem(part + d, row_parts)
        return p, pl.ds(pl.multiple_of(p * rows, 128), rows)

    def turn_part(tick, group, inner):
        size = math.gcd(inner.size, 768)

        @pl.loop(0, inner.size // size)
        def _(i):
            for way in range(2):
                block = current[tick, group, way, piece(i, size, inner.start), :].astype(jnp.float32)
                turned[way, piece(i, size), :] = turn(block).astype(jnp.bfloat16)

    ways = ((0, has_below, layer + 1), (1, has_above, layer - 1))

    def sender(way):
        return layer - 1 if way == 0 else layer + 1

    def crosses_early(step, way, sender):
        if not early:
            return jnp.bool_(False)
        rank = sender if way == 0 else layers - 1 - sender
        last = sum((rank == r).astype(jnp.int32) * count for r, count in early)
        return jnp.logical_and(step >= 0, step < last)

    def relay(step, i, into_last=False):
        if not early:
            return
        held_back, _, relay_send, relay_recv = relay_refs
        span = piece(i, big)
        for way, present, other in ways:
            @pl.when(crosses_early(step, way, layer))
            def _():
                ref = held_back.at[step, span, :]
                pltpu.make_async_copy(ref, ref, relay_recv.at[step, i]).wait()
                pltpu.make_async_remote_copy(
                    src_ref=ref,
                    dst_ref=current.at[step // 2 + 1, step % 2, way, piece(i, big, (1 - part) * rows), :],
                    send_sem=relay_send.at[step],
                    recv_sem=block_recv.at[way, i, 1 - part] if into_last else recv_sem.at[step // 2 + 1, step % 2, way, 1 - part],
                    device_id=(other, part),
                    device_id_type=MESH,
                ).start()

    def own_half(tick, group, relays=True):
        _, inner = part_of(0)
        turn_part(tick, group, inner)

        @pl.loop(0, rows // big)
        def _(i):
            step = 2 * tick + group

            @pl.when(step == 0)
            def _():
                load(i).wait()
            total[group, piece(i, big), :] = product(tick, group, piece(i, big), inner)
            if relays:
                relay(step - 2, i)

    def leave(tick, group, span, inner):
        out = product(tick, group, span, inner) + total[group, span, :]
        for way in range(2):
            value = out[:, way * lanes:(way + 1) * lanes] + source_term[group, way, span, :].astype(jnp.float32)
            if isinstance(tick, int) and tick == LAST:
                stage[span, way * lanes:(way + 1) * lanes] = value.astype(jnp.bfloat16)
            else:
                outgoing[2 * tick + group, way, span, :] = value.astype(jnp.bfloat16)

    def other_half(tick, group):
        for d in range(1, row_parts):
            p, inner = part_of(d)
            for way, present in ((0, has_above), (1, has_below)):
                @pl.when(jnp.logical_or(tick == 0, present))
                def _():
                    arrived(tick, group, way, p)
            turn_part(tick, group, inner)
            if d < row_parts - 1:
                @pl.loop(0, rows // big)
                def _(i):
                    span = piece(i, big)
                    total[group, span, :] += product(tick, group, span, inner)
                continue

            @pl.loop(0, chunks)
            def _(i):
                span = piece(i, chunk)
                leave(tick, group, span, inner)
                send_next(2 * tick + group, span, piece(i, chunk, own_base), i)

    def send_next(step, span, there, i):
        tick, group = step // 2, step % 2
        for way, present, other in ways:
            @pl.when(present)
            def _():
                pltpu.make_async_remote_copy(
                    src_ref=outgoing.at[step, way, span, :],
                    dst_ref=current.at[tick + 1, group, way, there, :],
                    send_sem=send_sem.at[step, way],
                    recv_sem=recv_sem.at[tick + 1, group, way, part],
                    device_id=(other, part),
                    device_id_type=MESH,
                ).start()

            if early:
                held_back, early_send, _, relay_recv = relay_refs

                @pl.when(crosses_early(step, way, layer))
                def _():
                    pltpu.make_async_remote_copy(
                        src_ref=outgoing.at[step, way, span, :],
                        dst_ref=held_back.at[step, span, :],
                        send_sem=early_send.at[step],
                        recv_sem=relay_recv.at[step, i // (big // chunk)],
                        device_id=(layer, 1 - part),
                        device_id_type=MESH,
                    ).start()

    def send_final(step, span):
        for way, present, other in ways:
            @pl.when(present)
            def _():
                pltpu.make_async_remote_copy(
                    src_ref=stage.at[span, way * lanes:(way + 1) * lanes],
                    dst_ref=final.at[way, span, :],
                    send_sem=send_sem.at[step, way],
                    recv_sem=final_sem.at[way],
                    device_id=(other, part),
                    device_id_type=MESH,
                ).start()

    def take_next(step):
        tick, group = step // 2, step % 2
        for way, present in ((0, has_above), (1, has_below)):
            @pl.when(jnp.logical_and(present, step >= 2))
            def _():
                arrived(tick, group, way, part)

                @pl.when(jnp.logical_not(crosses_early(step - 2, way, sender(way))))
                def _():
                    forward(tick, group, way, own)

    def take_last():
        for way, present in ((0, has_above), (1, has_below)):
            @pl.when(present)
            def _():
                arrived(LAST, 0, way, part)

                @pl.when(jnp.logical_not(crosses_early(2 * LAST - 2, way, sender(way))))
                def _():
                    for k in range(rows // big):
                        forward(LAST, 0, way, piece(k, big, own_base), block_recv.at[way, k, part])

    def other_last(pairs):
        for d, k in pairs:
            p = lax.rem(part + d, row_parts)
            inner = piece(k, big, p * rows)
            for way, present in ((0, has_above), (1, has_below)):
                @pl.when(present)
                def _():
                    ref = current.at[LAST, 0, way, inner, :]
                    pltpu.make_async_copy(ref, ref, block_recv.at[way, k, p]).wait()
            turn_part(LAST, 0, inner)
            final_block = d == row_parts - 1 and k == rows // big - 1

            for i in range(rows // tall):
                span = piece(i, tall)
                if final_block:
                    leave(LAST, 0, span, inner)
                    send_final(2 * LAST, span)
                else:
                    total[0, span, :] += product(LAST, 0, span, inner)

    def take_sub():
        for way, present in ((0, has_above), (1, has_below)):
            @pl.when(present)
            def _():
                arrived(LAST, 1, way, part)
                forward(LAST, 1, way, piece(0, joint, own_base))

        @pl.loop(0, (rows - joint) // deep)
        def _(i):
            span = piece(i, deep, own_base + joint)
            down = current[LAST, 1, 0, span, :].astype(jnp.float32)
            up = current[LAST, 1, 1, span, :].astype(jnp.float32)
            for q, block in enumerate(swap_quarters(down, up)):
                sub[q, span, :] = block.astype(jnp.bfloat16)

        for q in range(2):
            for k, (start, size) in enumerate(blocks[q]):
                for d in range(1, row_parts):
                    span = pl.ds(pl.multiple_of(own_base + start, 128), size)
                    pltpu.make_async_remote_copy(
                        src_ref=sub.at[q, span, :],
                        dst_ref=sub.at[q, span, :],
                        send_sem=sub_send.at[q, d - 1],
                        recv_sem=sub_recv.at[q, k, part],
                        device_id=(layer, lax.rem(part + d, row_parts)),
                        device_id_type=MESH,
                    ).start()

    def own_sub():
        _, inner = part_of(0)
        turn_part(LAST, 1, inner)

        @pl.loop(0, rows // big)
        def _(i):
            span = piece(i, big)
            out = product(LAST, 1, span, inner)
            sides = [
                out[:, way * lanes:(way + 1) * lanes] + source_term[1, way, span, :].astype(jnp.float32)
                for way in range(2)
            ]
            for q, block in enumerate(swap_quarters(*sides)):
                total[1, span, q * lanes:(q + 1) * lanes] = block

    def joint_sub():
        for d in range(1, row_parts):
            p = lax.rem(part + d, row_parts)
            inner = piece(0, joint, p * rows)
            for way, present in ((0, has_above), (1, has_below)):
                @pl.when(present)
                def _():
                    ref = current.at[LAST, 1, way, inner, :]
                    pltpu.make_async_copy(ref, ref, recv_sem.at[LAST, 1, way, p]).wait()
            turn_part(LAST, 1, inner)

            for i in range(rows // tall):
                span = piece(i, tall)
                out = product(LAST, 1, span, inner)
                for q, block in enumerate(swap_quarters(out[:, :lanes], out[:, lanes:])):
                    total[1, span, q * lanes:(q + 1) * lanes] += block

    def other_sub(q):
        for d in range(1, row_parts):
            p = lax.rem(part + d, row_parts)
            for k, (start, size) in enumerate(blocks[q]):
                inner = pl.ds(pl.multiple_of(p * rows + start, 128), size)
                ref = sub.at[q, inner, :]
                pltpu.make_async_copy(ref, ref, sub_recv.at[q, k, p]).wait()

                @pl.loop(0, size // deep)
                def _(i):
                    block = sub[q, piece(i, deep, p * rows + start), :].astype(jnp.float32)
                    swapped = exchange_quarters(block)
                    for n, value in enumerate((turn(block), swapped, turn(swapped))):
                        turned[n // 2, piece(i, deep, n % 2 * left), :] = value.astype(jnp.bfloat16)

                def product_sub(span):
                    columns = [sub[q, inner, :]] + [turned[n // 2, pl.ds(n % 2 * left, size), :] for n in range(3)]
                    return multiply(span, inner, columns) + total[1, span, q * lanes:(q + 1) * lanes]

                if d < row_parts - 1 or k < len(blocks[q]) - 1:
                    for i in range(rows // tall):
                        span = piece(i, tall)
                        total[1, span, q * lanes:(q + 1) * lanes] = product_sub(span)
                    continue

                for i in range(rows // slim):
                    out = product_sub(piece(i, slim))
                    here = piece(i, pair)
                    for (way, present, other), block in zip(ways, swap_quarters(out[:pair], out[pair:])):
                        ours, at = piece(i, pair, q * (rows // 2)), (2 + way) * lanes
                        stage[ours, at:at + lanes] = block.astype(jnp.bfloat16)

                        @pl.when(present)
                        def _():
                            pltpu.make_async_remote_copy(
                                src_ref=stage.at[ours, at:at + lanes],
                                dst_ref=final_sub.at[q, way, here, :],
                                send_sem=last_send.at[q, way],
                                recv_sem=last_recv.at[q, way],
                                device_id=(other, part),
                                device_id_type=MESH,
                            ).start()

    @pl.loop(0, 2 * LAST - 1)
    def _(step):
        tick, group = step // 2, step % 2
        own_half(tick, group)
        take_next(step + 1)
        other_half(tick, group)

    own_half(LAST - 1, 1)
    take_last()
    own_half(LAST, 0, False)
    other_half(LAST - 1, 1)
    pairs = [(d, k) for d in range(1, row_parts) for k in range(rows // big)]
    ahead = max(rows // big - 1, 0)
    for i in range(rows // big):
        relay(2 * LAST - 2, i, True)
    other_last(pairs[:1])
    take_sub()
    other_last(pairs[1:ahead])
    own_sub()
    other_last(pairs[ahead:])
    joint_sub()
    for q in range(2):
        other_sub(q)

    def whole(ref, sem):
        pltpu.make_async_copy(ref, ref, sem).wait()

    for way, came, goes in ((0, has_above, has_below), (1, has_below, has_above)):
        def sent(tick, group):
            for d in range(1, row_parts):
                whole(current.at[tick, group, way, own, :], row_send.at[tick, group, way, d - 1])

        for group in range(2):
            sent(0, group)

        @pl.when(came)
        def _():
            for step in range(2, 2 * LAST + 1):
                @pl.when(jnp.logical_not(crosses_early(step - 2, way, sender(way))))
                def _():
                    sent(step // 2, step % 2)
            if joint:
                for d in range(1, row_parts):
                    whole(current.at[LAST, 1, way, piece(0, joint, own_base), :], row_send.at[LAST, 1, way, d - 1])
            whole(final.at[way], final_sem.at[way])
            for q in range(2):
                whole(final_sub.at[q, way], last_recv.at[q, way])

        @pl.when(jnp.logical_not(came))
        def _():
            for copy in zero_final(way):
                copy.wait()

        @pl.when(goes)
        def _():
            for step in range(2 * LAST + 1):
                whole(outgoing.at[0, way], send_sem.at[step, way])
            for q in range(2):
                whole(outgoing.at[0, way, pl.ds(0, rows // 2), :], last_send.at[q, way])

        if early:
            for step in range(2 * LAST - 1):
                @pl.when(crosses_early(step, way, layer))
                def _():
                    for sem in relay_refs[1:3]:
                        whole(outgoing.at[step, way], sem.at[step])

    for q in range(2):
        for d in range(1, row_parts):
            whole(sub.at[q, piece(0, rows - joint, own_base + joint), :], sub_send.at[q, d - 1])


def unpack(chunk, slim, final, final_sub, result, first, second, natural, first_sem, second_sem, out_sem):
    rows, lanes = first.shape[1], first.shape[2]
    pair = chunk // 2
    chunks = rows // chunk

    def takes(i):
        full, half = pl.ds(i * chunk, chunk), pl.ds(i * pair, pair)
        return (
            pltpu.make_async_copy(final.at[:, full, :], first.at[:, full, :], first_sem.at[i]),
            pltpu.make_async_copy(final_sub.at[:, :, half, :], second.at[:, :, half, :], second_sem.at[i]),
        )

    def put(i):
        full = pl.ds(i * chunk, chunk)
        return pltpu.make_async_copy(natural.at[full, :], result.at[0, full, :], out_sem.at[i])

    for i in range(chunks):
        for copy in takes(i):
            copy.start()
    for i in range(chunks):
        for copy in takes(i):
            copy.wait()
        full, half = pl.ds(i * chunk, chunk), pl.ds(i * pair, pair)
        for way in range(2):
            a = first[way, full, :].astype(jnp.float32)
            parts = []
            for j in range(chunk // slim):
                short = pl.ds(i * pair + j * (slim // 2), slim // 2)
                parts += swap_quarters(*(second[q, way, short, :].astype(jnp.float32) for q in range(2)))
            b = jnp.concatenate(parts, 0)
            for n, block in enumerate(swap_halves(a, b)):
                at = (2 * way + n) * lanes
                natural[full, at:at + lanes] = block.astype(jnp.bfloat16)
        put(i).start()
    for i in range(chunks):
        put(i).wait()


def level(layers):
    chips = layers // 2
    counts = [(2 * i + 1, min(2 * LAST - 1, 4 - 8 * (i + 1) // chips)) for i in range(chips // 2 - 1)]
    return tuple((rank, count) for rank, count in counts if count > 0)


def per_device(waves, operators, sources, source_layer):
    layers, row_parts = lax.axis_size("layer"), lax.axis_size("row")
    rows, depth = operators.shape[2], operators.shape[3]
    lanes = waves.shape[2] // 4
    fine, chunk, big, tall, slim, deep, broad = (math.gcd(rows, size) for size in (256, 512, 512, 256, 256, 384, 512))
    deep = deep if deep < rows else math.gcd(rows, 128)
    joint = rows // deep // 2 * deep
    early = ()
    pieces, steps = rows // broad, 2 * LAST + 1
    peers = row_parts - 1
    anywhere = pl.BlockSpec(memory_space=pl.ANY)
    dma = pltpu.SemaphoreType.DMA
    relays = 2 * LAST - 1
    relay_shapes = [
        pltpu.VMEM((relays, rows, lanes), jnp.bfloat16),
        dma((relays,)),
        dma((relays,)),
        dma((relays, rows // big)),
    ] if early else []
    final, final_sub = pl.pallas_call(
        functools.partial(kernel, layers, row_parts, fine, chunk, big, tall, slim, joint, deep, early),
        out_shape=(
            jax.ShapeDtypeStruct((2, rows, lanes), jnp.bfloat16),
            jax.ShapeDtypeStruct((2, 2, rows // 2, lanes), jnp.bfloat16),
        ),
        in_specs=[anywhere, anywhere, anywhere, pl.BlockSpec(memory_space=pltpu.VMEM)],
        out_specs=(anywhere, anywhere),
        scratch_shapes=[
            pltpu.VMEM((4, rows, depth), jnp.bfloat16),
            pltpu.VMEM((TICKS, 2, 2, depth, lanes), jnp.bfloat16),
            pltpu.VMEM((2, max(rows, 2 * (rows - joint)), lanes), jnp.bfloat16),
            pltpu.VMEM((2, rows, 2 * lanes), jnp.float32),
            pltpu.VMEM((steps - 1, 2, rows, lanes), jnp.bfloat16),
            pltpu.VMEM((2, 2, rows, lanes), jnp.bfloat16),
            pltpu.VMEM((rows, 4 * lanes), jnp.bfloat16),
            pltpu.VMEM((2, depth, lanes), jnp.bfloat16),
            dma((rows // fine,)),
            dma((1,)),
            dma((rows // big,)),
            dma((2, 3)),
            dma((TICKS, 2, 2, peers)),
            dma((steps, 2)),
            dma((TICKS, 2, 2, row_parts)),
            dma((2,)),
            dma((2, rows // big, row_parts)),
            dma((2, peers)),
            dma((2, (rows - joint) // deep, row_parts)),
            dma((2, 2)),
            dma((2, 2)),
            *relay_shapes,
        ],
        compiler_params=pltpu.CompilerParams(
            collective_id=0, has_side_effects=True, vmem_limit_bytes=67043328
        ),
    )(waves, operators, sources, source_layer.reshape(1, lanes))
    return pl.pallas_call(
        functools.partial(unpack, broad, slim),
        out_shape=jax.ShapeDtypeStruct(waves.shape, jnp.bfloat16),
        in_specs=[anywhere, anywhere],
        out_specs=anywhere,
        scratch_shapes=[
            pltpu.VMEM(final.shape, jnp.bfloat16),
            pltpu.VMEM(final_sub.shape, jnp.bfloat16),
            pltpu.VMEM((rows, 4 * lanes), jnp.bfloat16),
            dma((pieces,)),
            dma((pieces,)),
            dma((pieces,)),
        ],
    )(final, final_sub)


def solution(mesh):
    return jax.shard_map(
        per_device,
        mesh=mesh,
        in_specs=(P("layer", "row", None), P("layer", None, "row", None), P("row", None), P()),
        out_specs=P("layer", "row", None),
        check_vma=False,
    )
```

time: 124 us -> 119 us (0.960)
  Pallas kernels: 124 us -> 119 us
    pallas_call x2, Pallas kernels: 124 us -> 119 us  [the longest x1 116 us: per_device(): pl.pallas_call(functools.partial(kernel, layers, row_parts, fine, chunk,...]
where the time goes in v2:
time: 119 us
  Pallas kernels  119 us (100%)
    pallas_call x1, Pallas kernels, per_device(): pl.pallas_call(functools.partial(kernel, layers, row_parts, fine, chunk,...  116 us
    pallas_call x1, Pallas kernels, per_device(): pl.pallas_call(functools.partial(unpack, broad, slim), out_shape=jax.Shap...  2.94 us

profile of v2, /device:TPU:17, one launch (start us, length us, event | category | flops | bytes accessed | tf_op | source)
XLA Modules:
  0.0 119.0 jit_solution(14027565808991351508)
XLA Ops:
  0.0 115.9 %shard_map.46 = (bf16[2,1536,128]{2,1,0:T(8,128)(2,1)}, bf16[2,2,768,128]{3,2,1,0:T(8,128)(2,1)}) custom-call(bf16[1,1536,512]{2,1,0:T(8,128)(2,1)} %waves.1, bf16[1,4,1536,3072]{3,2,1,0:T(8,128)(2,1)} %operators.1, bf16[1536,512]{1,0:T(8,128)(2,1)} %sources.1, s32[1,128]{1,0:T(1,128)} %bitcast.1), custom_call_target="tpu_custom_call" | custom-call | tf_op jit(solution)/shard_map/pallas_call | solution.py:585
  115.9 2.9 %shard_map.47 = bf16[1,1536,512]{2,1,0:T(8,128)(2,1)} custom-call(bf16[2,1536,128]{2,1,0:T(8,128)(2,1)} %get-tuple-element.7.final, bf16[2,2,768,128]{3,2,1,0:T(8,128)(2,1)} %get-tuple-element.8.final_sub), custom_call_target="tpu_custom_call" | custom-call | tf_op jit(solution)/shard_map/pallas_call | solution.py:621

commit v3 on v2

--- a/solution.py
+++ b/solution.py
@@ -60,7 +60,7 @@
     pieces, chunks = rows // fine, rows // chunk
     pair = slim // 2
     unit = math.gcd(math.gcd(fine, pair), deep)
-    blocks = ([(joint, rows - joint)], [(start, deep) for start in range(joint, rows, deep)])
+    blocks = [[(start, deep) for start in range(joint, rows, deep)]] * 2
     left = rows - joint
     has_above, has_below = layer > 0, layer < layers - 1
 
@@ -85,9 +85,6 @@
         @pl.when(present)
         def _():
             pl.semaphore_signal(barrier, inc=1, device_id=(other, part), device_id_type=MESH)
-
-    for i in range(rows // big):
-        load(i).start()
 
     def packed(span):
         for way in range(2):
@@ -121,6 +118,9 @@
                 current[0, group, way, span, :] = groups[group].astype(jnp.bfloat16)
         forward(0, 0, 0, span)
         forward(0, 0, 1, span)
+
+    for i in range(rows // big):
+        load(i).start()
 
     own = piece(0, rows, own_base)
     forward(0, 1, 0, own)
@@ -464,9 +464,8 @@
         relay(2 * LAST - 2, i, True)
     other_last(pairs[:1])
     take_sub()
-    other_last(pairs[1:ahead])
     own_sub()
-    other_last(pairs[ahead:])
+    other_last(pairs[1:])
     joint_sub()
     for q in range(2):
         other_sub(q)
@@ -543,15 +542,15 @@
             copy.wait()
         full, half = pl.ds(i * chunk, chunk), pl.ds(i * pair, pair)
         for way in range(2):
-            a = first[way, full, :].astype(jnp.float32)
+            a = first[way, full, :]
             parts = []
             for j in range(chunk // slim):
                 short = pl.ds(i * pair + j * (slim // 2), slim // 2)
-                parts += swap_quarters(*(second[q, way, short, :].astype(jnp.float32) for q in range(2)))
+                parts += swap_quarters(*(second[q, way, short, :] for q in range(2)))
             b = jnp.concatenate(parts, 0)
             for n, block in enumerate(swap_halves(a, b)):
                 at = (2 * way + n) * lanes
-                natural[full, at:at + lanes] = block.astype(jnp.bfloat16)
+                natural[full, at:at + lanes] = block
         put(i).start()
     for i in range(chunks):
         put(i).wait()

time: 119 us -> 119 us (level)
  no operation moved by 1% of the time
where the time goes in v3:
time: 119 us
  Pallas kernels  118 us (99%)
    pallas_call x1, Pallas kernels, per_device(): pl.pallas_call(functools.partial(kernel, layers, row_parts, fine, chunk,...  115 us
    pallas_call x1, Pallas kernels, per_device(): pl.pallas_call(functools.partial(unpack, broad, slim), out_shape=jax.Shap...  2.96 us

profile of v3, /device:TPU:17, one launch (start us, length us, event | category | flops | bytes accessed | tf_op | source)
XLA Modules:
  0.0 118.6 jit_solution(17009700254957714198)
XLA Ops:
  0.0 115.5 %shard_map.46 = (bf16[2,1536,128]{2,1,0:T(8,128)(2,1)}, bf16[2,2,768,128]{3,2,1,0:T(8,128)(2,1)}) custom-call(bf16[1,1536,512]{2,1,0:T(8,128)(2,1)} %waves.1, bf16[1,4,1536,3072]{3,2,1,0:T(8,128)(2,1)} %operators.1, bf16[1536,512]{1,0:T(8,128)(2,1)} %sources.1, s32[1,128]{1,0:T(1,128)} %bitcast.1), custom_call_target="tpu_custom_call" | custom-call | tf_op jit(solution)/shard_map/pallas_call | solution.py:584
  115.5 3.0 %shard_map.47 = bf16[1,1536,512]{2,1,0:T(8,128)(2,1)} custom-call(bf16[2,1536,128]{2,1,0:T(8,128)(2,1)} %get-tuple-element.7.final, bf16[2,2,768,128]{3,2,1,0:T(8,128)(2,1)} %get-tuple-element.8.final_sub), custom_call_target="tpu_custom_call" | custom-call | tf_op jit(solution)/shard_map/pallas_call | solution.py:620
